TPU v7x, 32 devices: a whole 2x2x4 slice. The times are simulated.
32 devices in a mesh: ctx: 16 (over z, x, core), exp: 2 (over y).
Axes of the slice: x: 2, y: 2, z: 4, core: 2. Of those that a mesh axis runs over, the one named last changes fastest.
Arguments:
- resid: bfloat16 [2048, 2880], P(('ctx', 'exp')), may hold values from -3 to 3
- queries: bfloat16 [2048, 2048], P('ctx', 'exp'), may hold values from -8 to 8
- keys: bfloat16 [2048, 256], P('ctx'), may hold values from -8 to 8
- values: bfloat16 [2048, 256], P('ctx'), may hold values from -6 to 6
- sinks: float32 [32], P('exp'), may hold values from 0 to 6
- out_weight: bfloat16 [2048, 2880], P('exp'), may hold values from -0.125 to 0.125
- norm_gain: float32 [2880], replicated, may hold values from 0.5 to 1.5
- gate_weight: bfloat16 [16, 2880, 1536], P('ctx', None, 'exp'), may hold values from -0.109375 to 0.109375
- up_weight: bfloat16 [16, 2880, 1536], P('ctx', None, 'exp'), may hold values from -0.109375 to 0.109375
- down_weight: bfloat16 [16, 1536, 2880], P('ctx', 'exp'), may hold values from -0.15625 to 0.15625
- routes: int32 [2048, 4], P('ctx'), may hold values from 0 to 15, all different within a row; in each aligned block of 128 rows (0 to 127, 128 to 255, ...) at most 64 rows name the same one
- route_weights: float32 [2048, 4], P('ctx'), may hold values from 0.05 to 0.6
Outputs:
- block_out: bfloat16 [2048, 2880], P(('ctx', 'exp'))
Inputs may be any that keep to these rules, and one draw needn't show every extreme that they name: `routes`: in each aligned block of 128 rows no expert is named by more than 64 rows, a bound that some block reaches; a row names 4 different experts.
All inputs are finite; a program needn't handle non-finite values.
Results may differ from a plain program's by a relative error of at most 0.0085.
Values may be sent and summed in bfloat16 or wider, within the bound.
A program may use at most 128 MiB of HBM per device.

v0:
```python
import jax
import jax.numpy as jnp
from jax import lax
from jax.sharding import PartitionSpec as P

HD = 64
QH = 32
KVH = 4
TOP = 4
WIN = 128


NEG_FILL = -1e30
EPSILON = 1e-05


def shifted(array, axis, by):
    size = lax.axis_size(axis)
    pairs = [(i, i + by) for i in range(size) if 0 <= i + by < size]
    return lax.ppermute(array, axis, pairs)


def per_device(
    resid,
    queries,
    keys,
    values,
    sinks,
    out_weight,
    norm_gain,
    gate_weight,
    up_weight,
    down_weight,
    routes,
    route_weights,
):
    rows_here = queries.shape[0]
    local_heads = queries.shape[1] // HD
    per_group = QH // KVH
    kv_count = max(1, local_heads // per_group)
    head_reps = local_heads // kv_count
    exp_rank = lax.axis_index("exp")
    ctx_rank = lax.axis_index("ctx")
    kv_first = exp_rank * local_heads // per_group
    prior_keys, prior_values = shifted((keys, values), "ctx", 1)
    keys_ext = jnp.concatenate([prior_keys, keys], 0).reshape(rows_here + WIN, KVH, HD)
    values_ext = jnp.concatenate([prior_values, values], 0).reshape(rows_here + WIN, KVH, HD)
    keys_sel = lax.dynamic_slice_in_dim(keys_ext, kv_first, kv_count, 1)
    values_sel = lax.dynamic_slice_in_dim(values_ext, kv_first, kv_count, 1)
    query_four = queries.reshape(rows_here, kv_count, head_reps, HD)
    scores = jnp.einsum(
        "qgrd,kgd->grqk", query_four, keys_sel, preferred_element_type=jnp.float32
    ) * HD ** (-0.5)
    first_pos = ctx_rank * rows_here
    query_pos = first_pos + jnp.arange(rows_here, dtype=jnp.int32)
    key_pos = first_pos - WIN + jnp.arange(rows_here + WIN, dtype=jnp.int32)
    visible = (
        (key_pos[None, :] <= query_pos[:, None])
        & (key_pos[None, :] > query_pos[:, None] - WIN)
        & (key_pos[None, :] >= 0)
    )
    masked = jnp.where(visible[None, None], scores, NEG_FILL)
    sink_cols = sinks.reshape(kv_count, head_reps)[:, :, None]
    row_max = jnp.maximum(jnp.max(masked, axis=-1), sink_cols)
    exp_terms = jnp.where(visible[None, None], jnp.exp(masked - row_max[..., None]), 0.0)
    denominator = jnp.sum(exp_terms, axis=-1) + jnp.exp(sink_cols - row_max)
    soft_weights = (exp_terms / denominator[..., None]).astype(jnp.bfloat16)
    attended = jnp.einsum(
        "grqk,kgd->qgrd", soft_weights, values_sel, preferred_element_type=jnp.float32
    )
    attended = attended.reshape(rows_here, local_heads * HD).astype(jnp.bfloat16)
    projected = lax.psum_scatter(
        jnp.dot(attended, out_weight, preferred_element_type=jnp.float32),
        "exp",
        scatter_dimension=0,
        tiled=True,
    )
    after_attention = resid.astype(jnp.float32) + projected
    mean_square = jnp.mean(after_attention * after_attention, axis=-1, keepdims=True)
    normed = (after_attention * lax.rsqrt(mean_square + EPSILON) * norm_gain).astype(jnp.bfloat16)
    all_normed = lax.all_gather(normed, "exp", axis=0, tiled=True)
    n_experts = lax.axis_size("ctx")
    capacity = 2 * rows_here * TOP // n_experts
    width = all_normed.shape[1]
    flat_ids = routes.reshape(-1)
    one_hot = (flat_ids[:, None] == jnp.arange(n_experts, dtype=jnp.int32)[None, :]).astype(
        jnp.int32
    )
    rank_in = jnp.sum(jnp.cumsum(one_hot, axis=0) * one_hot, axis=1) - 1
    slot_index = flat_ids * capacity + rank_in
    token_of = jnp.arange(rows_here * TOP, dtype=jnp.int32) // TOP
    outgoing = (
        jnp.zeros((n_experts * capacity, width), jnp.bfloat16)
        .at[slot_index]
        .set(all_normed[token_of])
    )
    outgoing = outgoing.reshape(n_experts, capacity, width)
    gate_local = gate_weight[0]
    up_local = up_weight[0]
    down_local = down_weight[0]
    slot_block = lax.all_to_all(outgoing, "ctx", split_axis=0, concat_axis=0, tiled=True)
    block_shape = slot_block.shape
    flat_rows = slot_block.reshape(-1, block_shape[2])
    gate_val = jnp.dot(flat_rows, gate_local, preferred_element_type=jnp.float32)
    up_val = jnp.dot(flat_rows, up_local, preferred_element_type=jnp.float32)
    activated = (jax.nn.silu(gate_val) * up_val).astype(jnp.bfloat16)
    partial_rows = jnp.dot(activated, down_local, preferred_element_type=jnp.float32).astype(
        jnp.bfloat16
    )
    partial_out = partial_rows.reshape(block_shape)
    returned = lax.all_to_all(partial_out, "ctx", split_axis=0, concat_axis=0, tiled=True)
    flat_back = returned.reshape(n_experts * capacity, width)
    picked = flat_back[slot_index].reshape(rows_here, TOP, width)
    combined = jnp.sum(picked.astype(jnp.float32) * route_weights[:, :, None], axis=1)
    expert_mix = lax.psum_scatter(
        combined.astype(jnp.bfloat16), "exp", scatter_dimension=0, tiled=True
    ).astype(jnp.float32)
    return (after_attention + expert_mix).astype(jnp.bfloat16)


def solution(mesh):
    in_specs = (
        P(("ctx", "exp"), None),
        P("ctx", "exp"),
        P("ctx", None),
        P("ctx", None),
        P("exp"),
        P("exp", None),
        P(),
        P("ctx", None, "exp"),
        P("ctx", None, "exp"),
        P("ctx", "exp", None),
        P("ctx", None),
        P("ctx", None),
    )
    out_specs = P(("ctx", "exp"), None)
    return jax.shard_map(
        per_device, mesh=mesh, in_specs=in_specs, out_specs=out_specs, check_vma=False
    )
```

profile of v0, /device:TPU:10, one launch (start us, length us, event | category | flops | bytes accessed | tf_op | source)
XLA Modules:
  0.0 438.7 jit_solution(13573109594631216473)
XLA Ops:
  6.5 0.0 copy-start.3
  6.5 0.0 reduce-scatter.3.cloned.1.call-start
  6.5 2.0 collective-permute-start.1
  8.6 3.6 collective-permute-start
  12.2 0.1 and_and_fusion
  12.4 1.1 copy.21
  13.5 0.7 max.17
  14.2 0.0 collective-permute-done.1
  14.2 0.8 pad_maximum_fusion.1
  15.1 0.1 copy.20
  15.2 0.5 fusion.12
  15.7 0.1 broadcast_maximum_fusion
  15.8 0.5 fusion.14
  16.3 0.1 exponential_add_fusion
  16.3 0.0 collective-permute-done
  16.4 0.0 copy-done.3
  16.4 0.1 copy.19
  16.5 0.7 convolution_convert_fusion.1
  17.2 0.0 copy-start.5
  17.2 0.0 copy-start.2
  17.2 6.0 %fusion.29 = f32[128,2880]{1,0:T(8,128)} fusion(bf16[128,1024]{0,1:T(8,128)(2,1)S(1)} %bitcast.75, bf16[1024,2880]{0,1:T(8,128)(2,1)} %param.17), kind=kOutput, calls=%fused_computation.64 | convolution fusion | flops 754974720 | bytes 7634944 | tf_op jit(solution)/shard_map/dot_general | solution.py:73
  23.2 0.0 copy-start.4
  23.2 0.0 reduce-scatter.3.cloned.1.call-update
  23.2 0.0 copy-done.5
  23.2 0.1 copy.24
  23.3 0.1 eq.29
  23.4 0.1 eq.25
  23.6 1.2 reduce-window.6
  24.7 0.2 slice_reduce_fusion
  25.0 0.1 copy.23
  25.1 0.1 mul.75
  25.2 0.1 fusion.21
  25.4 23.6 %reduce-scatter.3.cloned.1.call-done = f32[64,2880]{1,0:T(8,128)} async-done(((f32[128,2880]{1,0:T(8,128)}), f32[64,2880]{1,0:T(8,128)}) %reduce-scatter.3.cloned.1.call-update) | async-done | bytes 737296 | tf_op jit(solution)/shard_map/reduce_scatter | solution.py:72
  49.0 0.0 copy-done.2
  49.0 1.3 multiply_reduce_fusion.1
  50.3 0.0 copy-done.4
  50.3 1.3 multiply_convert_fusion.1
  51.6 11.5 %all_gather.3 = bf16[128,2880]{1,0:T(8,128)(2,1)S(1)} all-gather(bf16[64,2880]{1,0:T(8,128)(2,1)S(1)} %multiply_convert_fusion.1), channel_id=1, replica_groups=mesh['ctx'=16,'exp'=2] {'exp'}, dimensions={0}, use_global_device_ids=true | all-gather | bytes 1105920 | tf_op jit(solution)/shard_map/all_gather | solution.py:81
  63.1 17.5 %scatter_custom_fusion = bf16[1024,2880]{1,0:T(8,128)(2,1)} fusion(s32[512]{0:T(512)S(1)} %bitcast.77, bf16[128,2880]{1,0:T(8,128)(2,1)S(1)} %all_gather.3, s32[1024]{0:T(1024)S(1)} %pad_clamp_fusion.1, bf16[]{:T(256)} %constant.72.clone.1), kind=kCustom, calls=%fused_computation.11 | custom fusion | bytes 5898242 | tf_op jit(solution)/shard_map/scatter | solution.py:95
  80.6 137.5 %all_to_all.10 = bf16[16,64,2880]{2,1,0:T(8,128)(2,1)S(1)} all-to-all(bf16[16,64,2880]{2,1,0:T(8,128)(2,1)} %bitcast.70), channel_id=1, replica_groups=mesh['ctx'=16,'exp'=2] {'ctx'}, dimensions={0} | all-to-all | bytes 11796480 | tf_op jit(solution)/shard_map/all_to_all | solution.py:101
  218.2 0.0 copy-start.1
  218.2 2.6 copy-done.1
  220.7 9.0 %fusion.1 = f32[1024,768]{1,0:T(8,128)} fusion(bf16[1024,2880]{1,0:T(8,128)(2,1)S(1)} %bitcast.71, bf16[1,2880,768]{2,1,0:T(8,128)(2,1)} %param.20), kind=kOutput, calls=%fused_computation.6 | convolution fusion | flops 4529848320 | bytes 13467648 | tf_op jit(solution)/shard_map/dot_general | solution.py:105
  229.8 16.5 %convolution_convert_fusion = bf16[1024,2880]{0,1:T(8,128)(2,1)} fusion(bf16[1,768,2880]{1,2,0:T(8,128)(2,1)} %param.21, f32[1024,768]{1,0:T(8,128)} %fusion.1, bf16[1024,2880]{1,0:T(8,128)(2,1)} %bitcast.72, bf16[1,2880,768]{2,1,0:T(8,128)(2,1)} %param.19), kind=kOutput, calls=%fused_computation.4 | convolution fusion | flops 9067364352 | bytes 23789568 | tf_op jit(solution)/shard_map/dot_general | solution.py:107
  246.3 8.5 %copy.27 = bf16[1024,2880]{1,0:T(8,128)(2,1)} copy(bf16[1024,2880]{0,1:T(8,128)(2,1)} %convolution_convert_fusion) | data formatting | bytes 11796480 | tf_op jit(solution)/shard_map/convert_element_type | solution.py:107
  254.8 0.0 copy-start.6
  254.8 5.8 %all-to-all-start.1 = ((bf16[16,64,2880]{2,1,0:T(8,128)(2,1)}), bf16[16,64,2880]{2,1,0:T(8,128)(2,1)}, u32[]{:S(2)}, u32[]{:S(2)}) async-start(bf16[16,64,2880]{2,1,0:T(8,128)(2,1)} %bitcast.69), calls=%async_computation.2 | async-start | bytes 12058624 | tf_op jit(solution)/shard_map/all_to_all | solution.py:111
  260.7 0.0 reduce-scatter.5.cloned.1.call-start
  260.7 0.0 copy-done.6
  260.7 0.1 copy.28
  260.8 131.4 %all-to-all-done.1 = bf16[16,64,2880]{2,1,0:T(8,128)(2,1)} async-done(((bf16[16,64,2880]{2,1,0:T(8,128)(2,1)}), bf16[16,64,2880]{2,1,0:T(8,128)(2,1)}, u32[]{:S(2)}, u32[]{:S(2)}) %all-to-all-start.1) | async-done | bytes 5898272 | tf_op jit(solution)/shard_map/all_to_all | solution.py:111
  392.2 9.6 %gather_fusion = bf16[512,2880]{1,0:T(8,128)(2,1)S(1)} fusion(bf16[1024,2880]{1,0:T(8,128)(2,1)} %bitcast.20, s32[1024]{0:T(1024)S(1)} %pad_clamp_fusion), kind=kCustom, calls=%fused_computation.1 | custom fusion | bytes 5900288 | tf_op jit(solution)/shard_map/gather | solution.py:113
  401.8 3.6 reshape.235
  405.3 0.0 copy-start
  405.4 8.0 %multiply_reduce_fusion = bf16[128,2880]{1,0:T(8,128)(2,1)} fusion(f32[128,4,2880]{2,1,0:T(4,128)} %reshape.235, f32[128,4]{1,0:T(8,128)S(1)} %copy.28), kind=kLoop, calls=%fused_computation.3 | loop fusion | flops 2580480 | bytes 6637568 | tf_op jit(solution)/shard_map/reduce_sum | solution.py:114
  413.4 0.0 reduce-scatter.5.cloned.1.call-update
  413.4 16.3 %reduce-scatter.5.cloned.1.call-done = bf16[64,2880]{1,0:T(8,128)(2,1)} async-done(((bf16[128,2880]{1,0:T(8,128)(2,1)}), bf16[64,2880]{1,0:T(8,128)(2,1)}) %reduce-scatter.5.cloned.1.call-update) | async-done | bytes 368656 | tf_op jit(solution)/shard_map/reduce_scatter | solution.py:115
  429.7 0.0 copy-done
  429.7 1.8 add_convert_fusion
  (14 shorter events, 0.1 us)
Async XLA Ops:
  6.5 9.8 %copy-start.3 = (bf16[128,256]{1,0:T(8,128)(2,1)S(1)}, bf16[128,256]{1,0:T(8,128)(2,1)}, u32[]{:S(2)}) copy-start(bf16[128,256]{1,0:T(8,128)(2,1)} %param.15) | copy-start | bytes 196612
  6.5 42.4 %reduce-scatter.3.cloned.1.call-start = ((), (), s32[]{:S(2)}) async-start(), calls=%async_computation.4 | async-start | bytes 2260992 | tf_op jit(solution)/shard_map/reduce_scatter | solution.py:72
  6.5 7.7 %collective-permute-start.1 = (bf16[128,256]{1,0:T(8,128)(2,1)}, bf16[128,256]{1,0:T(8,128)(2,1)S(1)}, u32[]{:S(2)}, u32[]{:S(2)}) collective-permute-start(bf16[128,256]{1,0:T(8,128)(2,1)} %param.14), channel_id=1, source_target_pairs={{0,2},{2,4},{4,6},{6,8},{8,10},{10,12},{12,14},{14,16},{16,18},{18... | collective-permute-start | bytes 196616 | tf_op jit(solution)/shard_map/ppermute | solution.py:20
  8.6 7.8 %collective-permute-start = (bf16[128,256]{1,0:T(8,128)(2,1)}, bf16[128,256]{1,0:T(8,128)(2,1)S(1)}, u32[]{:S(2)}, u32[]{:S(2)}) collective-permute-start(bf16[128,256]{1,0:T(8,128)(2,1)} %param.15), channel_id=1, source_target_pairs={{0,2},{2,4},{4,6},{6,8},{8,10},{10,12},{12,14},{14,16},{16,18},{18... | collective-permute-start | bytes 196616 | tf_op jit(solution)/shard_map/ppermute | solution.py:20
  17.2 6.0 %copy-start.5 = (s32[128,4]{0,1:T(4,128)S(1)}, s32[128,4]{0,1:T(4,128)}, u32[]{:S(2)}) copy-start(s32[128,4]{0,1:T(4,128)} %param.22) | copy-start | bytes 6148
  17.2 31.8 %copy-start.2 = (bf16[64,2880]{1,0:T(8,128)(2,1)S(1)}, bf16[64,2880]{1,0:T(8,128)(2,1)}, u32[]{:S(2)}) copy-start(bf16[64,2880]{1,0:T(8,128)(2,1)} %param.12) | copy-start | bytes 1105924
  23.2 27.1 %copy-start.4 = (f32[2880]{0:T(1024)S(1)}, f32[2880]{0:T(1024)}, u32[]{:S(2)}) copy-start(f32[2880]{0:T(1024)} %param.18) | copy-start | bytes 34564
  218.2 2.6 copy-start.1
  254.8 5.9 %copy-start.6 = (f32[128,4]{0,1:T(4,128)S(1)}, f32[128,4]{0,1:T(4,128)}, u32[]{:S(2)}) copy-start(f32[128,4]{0,1:T(4,128)} %param.23) | copy-start | bytes 6148
  254.8 137.4 %all-to-all-start.1 = ((bf16[16,64,2880]{2,1,0:T(8,128)(2,1)}), bf16[16,64,2880]{2,1,0:T(8,128)(2,1)}, u32[]{:S(2)}, u32[]{:S(2)}) async-start(bf16[16,64,2880]{2,1,0:T(8,128)(2,1)} %bitcast.69), calls=%async_computation.2 | async-start | bytes 12058624 | tf_op jit(solution)/shard_map/all_to_all | solution.py:111
  260.7 169.0 %reduce-scatter.5.cloned.1.call-start = ((), (), s32[]{:S(2)}) async-start(), calls=%async_computation.5 | async-start | bytes 1130496 | tf_op jit(solution)/shard_map/reduce_scatter | solution.py:115
  405.3 24.4 %copy-start = (f32[64,2880]{1,0:T(8,128)S(1)}, f32[64,2880]{1,0:T(8,128)}, u32[]{:S(2)}) copy-start(f32[64,2880]{1,0:T(8,128)} %reduce-scatter.3.cloned.1.call-done) | copy-start | bytes 2211844
Sparse Core Ops, SparseCore 0:
  23.3 25.5 reduce-scatter.2
  413.5 16.1 reduce-scatter.4
where the time goes:
time: 445 us; the launch traced here: 439 us
  waiting for transfers between devices  171 us (38%)
  blocking collectives  149 us (33%)
  local copies, waits for them, and re-layouts  44.7 us (10%)
  matrix products  32.8 us (7%)
  other arithmetic  15.4 us (3%)
  between operations  13.9 us (3%)
  starting transfers between devices  11.5 us (3%)
    all_to_all x1, blocking collectives, per_device(): lax.all_to_all(outgoing, 'ctx', split_axis=0, concat_axis=0, tiled=True)  138 us
    all_to_all x1, waiting for transfers between devices, per_device(): lax.all_to_all(partial_out, 'ctx', split_axis=0, concat_axis=0, tiled=True)  131 us
    reduce_scatter x1, waiting for transfers between devices, per_device(): lax.psum_scatter(jnp.dot(attended, out_weight, preferred_element_type=jnp...  23.6 us
    scatter x1, local copies, waits for them, and re-layouts, per_device(): outgoing = jnp.zeros((n_experts * capacity, width), jnp.bfloat16).at[slot...  17.5 us
    dot_general x1, matrix products, per_device(): jnp.dot(activated, down_local, preferred_element_type=jnp.float32)  16.5 us
    reduce_scatter x1, waiting for transfers between devices, per_device(): lax.psum_scatter(combined.astype(jnp.bfloat16), 'exp', scatter_dimension=...  16.3 us
    all_gather x1, blocking collectives, per_device(): all_normed = lax.all_gather(normed, 'exp', axis=0, tiled=True)  11.5 us
    gather x1, local copies, waits for them, and re-layouts, per_device(): picked = flat_back[slot_index].reshape(rows_here, TOP, width)  9.57 us
  transfers between devices with their start and end apart: 5, of which 3 were waited for; matrix products, arithmetic and copies ran while one was open for 1% of the time, Pallas kernels for 0%

commit v1 on v0

--- a/solution.py
+++ b/solution.py
@@ -18,6 +18,154 @@
     size = lax.axis_size(axis)
     pairs = [(i, i + by) for i in range(size) if 0 <= i + by < size]
     return lax.ppermute(array, axis, pairs)
+
+
+def flipped(array, bit):
+    size = lax.axis_size("ctx")
+    return lax.ppermute(array, "ctx", [(i, i ^ bit) for i in range(size)])
+
+
+def swapped(array):
+    return lax.ppermute(array, "exp", [(0, 1), (1, 0)])
+
+
+def paired(mine, other, position, axis):
+    low = jnp.where(position == 0, mine, other)
+    high = jnp.where(position == 0, other, mine)
+    return jnp.stack([low, high], axis)
+
+
+def sum_halves(rows, position):
+    half = rows.shape[0] // 2
+    kept = lax.dynamic_slice_in_dim(rows, position * half, half, 0)
+    sent = lax.dynamic_slice_in_dim(rows, (1 - position) * half, half, 0)
+    return kept + swapped(sent.astype(jnp.bfloat16)).astype(jnp.float32)
+
+
+def ranks(hit):
+    count = hit.shape[1]
+    places = jnp.arange(count)
+    before = (places[:, None] < places[None, :]).astype(jnp.bfloat16)
+    return jnp.dot(
+        hit.astype(jnp.bfloat16), before, preferred_element_type=jnp.float32
+    ).astype(jnp.int32)
+
+
+def per_device_grouped(
+    resid,
+    queries,
+    keys,
+    values,
+    sinks,
+    out_weight,
+    norm_gain,
+    gate_weight,
+    up_weight,
+    down_weight,
+    routes,
+    route_weights,
+):
+    rows_here = queries.shape[0]
+    local_heads = queries.shape[1] // HD
+    per_group = QH // KVH
+    kv_count = max(1, local_heads // per_group)
+    head_reps = local_heads // kv_count
+    exp_rank = lax.axis_index("exp")
+    ctx_rank = lax.axis_index("ctx")
+    kv_first = exp_rank * local_heads // per_group
+    prior_keys, prior_values = shifted((keys, values), "ctx", 1)
+    keys_ext = jnp.concatenate([prior_keys, keys], 0).reshape(rows_here + WIN, KVH, HD)
+    values_ext = jnp.concatenate([prior_values, values], 0).reshape(rows_here + WIN, KVH, HD)
+    keys_sel = lax.dynamic_slice_in_dim(keys_ext, kv_first, kv_count, 1)
+    values_sel = lax.dynamic_slice_in_dim(values_ext, kv_first, kv_count, 1)
+    query_four = queries.reshape(rows_here, kv_count, head_reps, HD)
+    scores = jnp.einsum(
+        "qgrd,kgd->grqk", query_four, keys_sel, preferred_element_type=jnp.float32
+    ) * HD ** (-0.5)
+    first_pos = ctx_rank * rows_here
+    query_pos = first_pos + jnp.arange(rows_here, dtype=jnp.int32)
+    key_pos = first_pos - WIN + jnp.arange(rows_here + WIN, dtype=jnp.int32)
+    visible = (
+        (key_pos[None, :] <= query_pos[:, None])
+        & (key_pos[None, :] > query_pos[:, None] - WIN)
+        & (key_pos[None, :] >= 0)
+    )
+    masked = jnp.where(visible[None, None], scores, NEG_FILL)
+    sink_cols = sinks.reshape(kv_count, head_reps)[:, :, None]
+    row_max = jnp.maximum(jnp.max(masked, axis=-1), sink_cols)
+    exp_terms = jnp.where(visible[None, None], jnp.exp(masked - row_max[..., None]), 0.0)
+    denominator = jnp.sum(exp_terms, axis=-1) + jnp.exp(sink_cols - row_max)
+    soft_weights = (exp_terms / denominator[..., None]).astype(jnp.bfloat16)
+    attended = jnp.einsum(
+        "grqk,kgd->qgrd", soft_weights, values_sel, preferred_element_type=jnp.float32
+    )
+    attended = attended.reshape(rows_here, local_heads * HD).astype(jnp.bfloat16)
+    width = out_weight.shape[1]
+    own_rows = rows_here // 2
+    n_experts = lax.axis_size("ctx")
+    capacity = 2 * rows_here * TOP // n_experts
+    table = jnp.concatenate([routes.astype(jnp.float32), route_weights], axis=1)
+    tables = lax.all_gather(table, "ctx", axis=0)
+    ids_all = tables[:, :, :TOP].astype(jnp.int32)
+    weights_all = tables[:, :, TOP:]
+    named = ids_all == ctx_rank
+    hit_here = jnp.any(named, axis=2)
+    weight_here = jnp.sum(jnp.where(named, weights_all, 0.0), axis=2)
+    slots = jnp.arange(capacity, dtype=jnp.int32)
+    pick = hit_here[:, None, :] & (ranks(hit_here)[:, None, :] == slots[None, :, None])
+    slot_weight = jnp.sum(jnp.where(pick, weight_here[:, None, :], 0.0), axis=2)
+    pick = pick.astype(jnp.bfloat16)
+    hit_mine = jnp.any(routes[None, :, :] == jnp.arange(n_experts)[:, None, None], axis=2)
+    place = hit_mine[:, :, None] & (ranks(hit_mine)[:, :, None] == slots[None, None, :])
+    place = place.transpose(1, 0, 2).reshape(rows_here, n_experts * capacity).astype(jnp.bfloat16)
+
+    projected = sum_halves(jnp.dot(attended, out_weight, preferred_element_type=jnp.float32), exp_rank)
+    after_attention = resid.astype(jnp.float32) + projected
+    mean_square = jnp.mean(after_attention * after_attention, axis=-1, keepdims=True)
+    normed = (after_attention * lax.rsqrt(mean_square + EPSILON) * norm_gain).astype(jnp.bfloat16)
+
+    core, x_pos, z_pos = ctx_rank % 2, ctx_rank // 2 % 2, ctx_rank // 4
+    by_z = [normed] * 4
+    for step in (1, -1):
+        moving = normed
+        for far in range(1, 4):
+            moving = shifted(moving, "ctx", 4 * step)
+            for z in range(4):
+                by_z[z] = jnp.where(z_pos - step * far == z, moving, by_z[z])
+    column = jnp.stack(by_z)
+    first, second = column[:, : own_rows // 2], column[:, own_rows // 2 :]
+    first = paired(first, flipped(first, 2), x_pos, 0)
+    first = paired(first, swapped(first), exp_rank, 0)
+    second = paired(second, swapped(second), exp_rank, 0)
+    second = paired(second, flipped(second, 2), x_pos, 0)
+    block = jnp.stack([first.transpose(2, 1, 0, 3, 4), second.transpose(2, 0, 1, 3, 4)], 3)
+    block = block.reshape(n_experts // 2, rows_here, width)
+
+    def expert_rows(tokens, owner):
+        chosen = lax.dynamic_index_in_dim(
+            pick.reshape(n_experts // 2, 2, capacity, rows_here), owner, 1, False
+        )
+        gains = lax.dynamic_index_in_dim(
+            slot_weight.reshape(n_experts // 2, 2, capacity), owner, 1, False
+        ).reshape(-1, 1)
+        rows_in = jnp.einsum(
+            "bst,btd->bsd", chosen, tokens, preferred_element_type=jnp.float32
+        ).astype(jnp.bfloat16).reshape(-1, width)
+        gate_val = jnp.dot(rows_in, gate_weight[0], preferred_element_type=jnp.float32)
+        up_val = jnp.dot(rows_in, up_weight[0], preferred_element_type=jnp.float32)
+        activated = (jax.nn.silu(gate_val) * up_val).astype(jnp.bfloat16)
+        rows_out = jnp.dot(activated, down_weight[0], preferred_element_type=jnp.float32)
+        return (rows_out * gains).astype(jnp.bfloat16).reshape(-1, capacity, width)
+
+    other = flipped(block, 1)
+    mine_out = expert_rows(block, core)
+    other_out = expert_rows(other, 1 - core)
+    outgoing = paired(mine_out, other_out, core, 1).reshape(n_experts, capacity, width)
+    returned = lax.all_to_all(outgoing, "ctx", split_axis=0, concat_axis=0, tiled=True)
+    combined = jnp.dot(
+        place, returned.reshape(n_experts * capacity, width), preferred_element_type=jnp.float32
+    )
+    return (after_attention + sum_halves(combined, exp_rank)).astype(jnp.bfloat16)
 
 
 def per_device(
@@ -134,6 +282,8 @@
         P("ctx", None),
     )
     out_specs = P(("ctx", "exp"), None)
+    grouped = mesh.shape["ctx"] == 16 and mesh.shape["exp"] == 2
+    body = per_device_grouped if grouped else per_device
     return jax.shard_map(
-        per_device, mesh=mesh, in_specs=in_specs, out_specs=out_specs, check_vma=False
-    )
+        body, mesh=mesh, in_specs=in_specs, out_specs=out_specs, check_vma=False
+    )

time: 445 us -> 426 us (0.957)
  blocking collectives: 149 us -> 19 us
  local copies, waits for them, and re-layouts: 44.7 us -> 76.6 us
  starting transfers between devices: 11.5 us -> 43 us
  waiting for transfers between devices: 171 us -> 197 us
  matrix products: 32.8 us -> 50.8 us
  other arithmetic: 15.4 us -> 32.7 us
  between operations: 13.9 us -> 1 us
    all_to_all x1 -> x0, blocking collectives: 138 us -> none  [per_device(): lax.all_to_all(outgoing, 'ctx', split_axis=0, concat_axis=0, tiled=True)]
    ppermute x0 -> x7, waiting for transfers between devices: none -> 54.7 us  [the longest x3 30.2 us: flipped(): return lax.ppermute(array, 'ctx', [(i, i ^ bit) for i in range(size)])]
    reduce_scatter x2 -> x0, waiting for transfers between devices: 39.9 us -> none  [the longest x1 23.6 us: per_device(): lax.psum_scatter(jnp.dot(attended, out_weight, preferred_element_type=jnp...]
    another operation x2 -> x11, other arithmetic: 1.19 us -> 25.1 us  [the longest x6 16 us: paired(): return jnp.stack([low, high], axis)]
    ppermute x0 -> x10, local copies, waits for them, and re-layouts: none -> 20.2 us  [the longest x6 9.31 us: shifted(): return lax.ppermute(array, axis, pairs)]
    ppermute x2 -> x8, starting transfers between devices: 5.6 us -> 24.6 us  [shifted(): return lax.ppermute(array, axis, pairs)]
    dot_general x5 -> x12, matrix products: 32.8 us -> 50.8 us  [the longest x2 24.2 us: expert_rows(): jnp.dot(activated, down_weight[0], preferred_element_type=jnp.float32)]
    scatter x1 -> x0, local copies, waits for them, and re-layouts: 17.5 us -> none  [per_device(): outgoing = jnp.zeros((n_experts * capacity, width), jnp.bfloat16).at[slot...]
  transfers between devices with their start and end apart: 5 -> 16, of which waited for: 3 -> 8; matrix products, arithmetic and copies ran while one was open for 1% -> 9% of each run, Pallas kernels for 0% -> 0%
where the time goes in v1:
time: 426 us; the launch traced here: 420 us
  waiting for transfers between devices  197 us (46%)
  local copies, waits for them, and re-layouts  76.6 us (18%)
  matrix products  50.8 us (12%)
  starting transfers between devices  43 us (10%)
  other arithmetic  32.7 us (8%)
  blocking collectives  19 us (4%)
    all_to_all x1, waiting for transfers between devices, per_device_grouped(): lax.all_to_all(outgoing, 'ctx', split_axis=0, concat_axis=0, tiled=True)  131 us
    ppermute x3, waiting for transfers between devices, flipped(): return lax.ppermute(array, 'ctx', [(i, i ^ bit) for i in range(size)])  30.2 us
    ppermute x8, starting transfers between devices, shifted(): return lax.ppermute(array, axis, pairs)  24.6 us
    ppermute x4, waiting for transfers between devices, swapped(): return lax.ppermute(array, 'exp', [(0, 1), (1, 0)])  24.5 us
    dot_general x2, matrix products, expert_rows(): jnp.dot(activated, down_weight[0], preferred_element_type=jnp.float32)  24.2 us
    all_gather x1, blocking collectives, per_device_grouped(): tables = lax.all_gather(table, 'ctx', axis=0)  19 us
    another operation x6, other arithmetic, paired(): return jnp.stack([low, high], axis)  16 us
    another operation x5, local copies, waits for them, and re-layouts, paired(): return jnp.stack([low, high], axis)  15.9 us
  transfers between devices with their start and end apart: 16, of which 8 were waited for; matrix products, arithmetic and copies ran while one was open for 9% of the time, Pallas kernels for 0%

profile of v1, /device:TPU:10, one launch (start us, length us, event | category | flops | bytes accessed | tf_op | source)
XLA Modules:
  0.0 419.6 jit_solution(4207577773166658031)
XLA Ops:
  0.0 1.9 collective-permute-start.1
  1.9 3.6 collective-permute-start
  12.9 1.7 fusion.52
  15.2 1.6 collective-permute-start.2
  16.8 1.2 copy.150
  18.0 8.0 %collective-permute-done.2 = bf16[64,2880]{1,0:T(8,128)(2,1)S(1)} collective-permute-done((bf16[64,2880]{1,0:T(8,128)(2,1)S(1)}, bf16[64,2880]{1,0:T(8,128)(2,1)S(1)}, u32[]{:S(2)}, u32[]{:S(2)}) %collective-permute-start.2) | collective-permute-done | bytes 368672 | tf_op jit(solution)/shard_map/ppermute | solution.py:29
  26.0 1.2 copy.156
  27.1 1.8 multiply_reduce_fusion
  30.4 3.5 collective-permute-start.6
  33.9 2.4 collective-permute-start.3
  36.3 6.1 %collective-permute-done.6 = bf16[64,2880]{1,0:T(8,128)(2,1)S(1)} collective-permute-done((bf16[64,2880]{1,0:T(8,128)(2,1)}, bf16[64,2880]{1,0:T(8,128)(2,1)S(1)}, u32[]{:S(2)}, u32[]{:S(2)}) %collective-permute-start.6) | collective-permute-done | bytes 368672 | tf_op jit(solution)/shard_map/ppermute | solution.py:20
  42.3 3.5 collective-permute-start.7
  45.8 3.1 collective-permute-start.4
  48.9 4.4 %collective-permute-done.7 = bf16[64,2880]{1,0:T(8,128)(2,1)} collective-permute-done((bf16[64,2880]{1,0:T(8,128)(2,1)S(1)}, bf16[64,2880]{1,0:T(8,128)(2,1)}, u32[]{:S(2)}, u32[]{:S(2)}) %collective-permute-start.7) | collective-permute-done | bytes 368672 | tf_op jit(solution)/shard_map/ppermute | solution.py:20
  53.3 3.5 collective-permute-start.8
  56.8 3.3 collective-permute-start.5
  60.9 2.1 copy.165
  63.0 2.2 copy.162
  65.2 2.1 copy.163
  67.3 2.1 copy.166
  69.5 2.8 select_bitcast_fusion.10
  72.3 1.4 select_bitcast_fusion.11
  74.5 3.5 fusion.49
  78.0 3.9 copy.185
  82.2 3.9 copy.190
  86.0 1.5 collective-permute-start.11
  87.5 10.3 %collective-permute-done.9 = bf16[4,32,2880]{2,1,0:T(8,128)(2,1)} collective-permute-done((bf16[4,32,2880]{2,1,0:T(8,128)(2,1)}, bf16[4,32,2880]{2,1,0:T(8,128)(2,1)}, u32[]{:S(2)}, u32[]{:S(2)}) %collective-permute-start.9) | collective-permute-done | bytes 737312 | tf_op jit(solution)/shard_map/ppermute | solution.py:25
  97.9 3.9 copy.186
  101.7 3.8 copy.191
  105.5 7.0 %select_bitcast_fusion.3 = (bf16[1,4,32,2880]{2,3,1,0:T(8,128)(2,1)}, bf16[1,4,32,2880]{2,3,1,0:T(8,128)(2,1)}, bf16[1,4,32,2880]{2,3,1,0:T(8,128)(2,1)}, bf16[1,4,32,2880]{2,3,1,0:T(8,128)(2,1)}) fusion(bf16[4,32,2880]{1,2,0:T(8,128)(2,1)} %copy.186, pred[]{:T(512)S(6)} %eq.160, bf16[4,64,2880]{1,2,0:T(8,128)(2,1)S(1)} %pad_maximum_fusion.2, ...), kind=kLoop, calls=%fused_computation.23 | loop fusion | flops 1474560 | bytes 5898242 | tf_op jit(solution)/shard_map/stack | solution.py:35
  112.5 4.0 copy.194
  116.5 2.5 copy.193
  119.0 2.9 pad_maximum_fusion.4
  121.9 1.7 collective-permute-start.12
  123.6 3.9 copy.188
  127.5 2.5 copy.189
  130.0 1.6 pad_maximum_fusion.3
  131.6 1.6 collective-permute-start.10
  133.2 19.9 %collective-permute-done.12 = bf16[2,4,32,2880]{3,2,1,0:T(8,128)(2,1)} collective-permute-done((bf16[2,4,32,2880]{3,2,1,0:T(8,128)(2,1)}, bf16[2,4,32,2880]{3,2,1,0:T(8,128)(2,1)}, u32[]{:S(2)}, u32[]{:S(2)}) %collective-permute-start.12) | collective-permute-done | bytes 1474592 | tf_op jit(solution)/shard_map/ppermute | solution.py:25
  153.1 1.7 select_bitcast_fusion.5
  155.2 6.9 %collective-permute-done.10 = bf16[2,4,32,2880]{3,2,1,0:T(8,128)(2,1)S(1)} collective-permute-done((bf16[2,4,32,2880]{3,2,1,0:T(8,128)(2,1)S(1)}, bf16[2,4,32,2880]{3,2,1,0:T(8,128)(2,1)S(1)}, u32[]{:S(2)}, u32[]{:S(2)}) %collective-permute-start.10) | collective-permute-done | bytes 1474592 | tf_op jit(solution)/shard_map/ppermute | solution.py:29
  162.4 3.8 pad_maximum_fusion
  166.2 8.4 %copy.198 = bf16[8,128,2880]{1,2,0:T(8,128)(2,1)} copy(bf16[8,128,2880]{2,1,0:T(8,128)(2,1)} %bitcast.120) | data formatting | bytes 11796480 | tf_op jit(solution)/shard_map/reshape | solution.py:142
  174.6 19.0 %all-gather = f32[2048,8]{0,1:T(8,128)S(1)} all-gather(f32[128,8]{0,1:T(8,128)S(1)} %pad_maximum_fusion.7), channel_id=2, replica_groups=mesh['ctx'=16,'exp'=2] {'ctx'}, dimensions={0}, use_global_device_ids=true | all-gather | bytes 69632 | tf_op jit(solution)/shard_map/all_gather | solution.py:108
  194.4 3.8 convolution_convert_fusion.1
  198.2 6.1 %fusion.8 = f32[512,768]{1,0:T(8,128)} fusion(bf16[512,2880]{1,0:T(8,128)(2,1)S(1)} %bitcast.127, bf16[1,2880,768]{2,1,0:T(8,128)(2,1)} %param.19), kind=kOutput, calls=%fused_computation.14 | convolution fusion | flops 2264924160 | bytes 8945664 | tf_op jit(solution)/shard_map/dot_general | solution.py:154
  204.3 4.6 %convolution_convert_fusion = bf16[8,64,2880]{2,1,0:T(8,128)(2,1)S(1)} fusion(bf16[8,128,2880]{1,2,0:T(8,128)(2,1)} %collective-permute-done.13, pred[8,2,64,128]{3,2,0,1:T(32,128)(4,1)S(1)} %fusion.22, s32[]{:T(128)S(6)} %select_n.354), kind=kOutput, calls=%fused_computation.4 | convolution fusion | flops 378961920 | bytes 8912900 | tf_op jit(solution)/shard_map/bst,btd->bsd/dot_general | solution.py:151
  208.9 1.6 copy-done.12
  210.5 3.8 fusion.6
  214.2 11.5 %multiply_convert_fusion = bf16[512,2880]{0,1:T(8,128)(2,1)} fusion(bf16[1,768,2880]{1,2,0:T(8,128)(2,1)} %param.21, f32[512]{0:T(512)S(1)} %mul.94, f32[512,768]{1,0:T(8,128)} %fusion.6, bf16[512,2880]{1,0:T(8,128)(2,1)} %bitcast.130, bf16[1,2880,768]{2,1,0:T(8,128)(2,1)} %param.20), kind=kOutput, calls=%fused_computation.2 | convolution fusion | flops 4535156736 | bytes 16320512 | tf_op jit(solution)/shard_map/dot_general | solution.py:157
  225.7 12.7 %broadcast_select_fusion.1 = (bf16[512,2880]{0,1:T(8,128)(2,1)}, bf16[512,2880]{0,1:T(8,128)(2,1)}) fusion(bf16[512,2880]{0,1:T(8,128)(2,1)} %multiply_convert_fusion, pred[]{:T(512)S(6)} %eq.152, f32[512]{0:T(512)S(1)} %mul.89, bf16[1,768,2880]{1,2,0:T(8,128)(2,1)} %param.21, f32[512,768]{1,0:T(8,128)} %fusion.8, bf16[512,2880]{1,0:T(8,128)(2,1)S(1)} %bitcast.128, ...), kind=kOutput, calls=%fused_computation.25 | convolution fusion | flops 4538105856 | bytes 22218752 | tf_op jit(solution)/shard_map/dot_general | solution.py:157
  238.4 3.3 copy.199
  241.8 4.6 %copy.200 = bf16[512,2880]{1,0:T(8,128)(2,1)} copy(bf16[512,2880]{0,1:T(8,128)(2,1)} %get-tuple-element.12) | data formatting | bytes 5898240 | tf_op jit(solution)/shard_map/jit(_where)/select_n | solution.py:34
  246.4 2.5 pad_maximum_fusion.1
  248.8 3.0 copy.201
  251.8 10.1 %all-to-all-start = ((bf16[16,64,2880]{2,1,0:T(8,128)(2,1)}), bf16[16,64,2880]{2,1,0:T(8,128)(2,1)}, u32[]{:S(2)}, u32[]{:S(2)}) async-start(bf16[16,64,2880]{2,1,0:T(8,128)(2,1)} %bitcast.122), calls=%async_computation | async-start | bytes 12058624 | tf_op jit(solution)/shard_map/all_to_all | solution.py:164
  262.1 131.4 %all-to-all-done = bf16[16,64,2880]{2,1,0:T(8,128)(2,1)} async-done(((bf16[16,64,2880]{2,1,0:T(8,128)(2,1)}), bf16[16,64,2880]{2,1,0:T(8,128)(2,1)}, u32[]{:S(2)}, u32[]{:S(2)}) %all-to-all-start) | async-done | bytes 5898272 | tf_op jit(solution)/shard_map/all_to_all | solution.py:164
  393.5 5.2 %convolution_bitcast_fusion = f32[128,2880]{0,1:T(8,128)S(1)} fusion(bf16[16,64,2880]{2,1,0:T(8,128)(2,1)} %all-to-all-done, s32[128,16]{0,1:T(8,128)S(1)} %convolution_convert_fusion.4, pred[128,16]{0,1:T(8,128)(4,1)S(1)} %bitcast.139), kind=kOutput, calls=%fused_computation.16 | convolution fusion | flops 755236864 | bytes 7383040 | tf_op jit(solution)/shard_map/dot_general | solution.py:165
  399.8 1.4 copy.210
  401.2 1.6 collective-permute-start.14
  402.8 9.6 %collective-permute-done.14 = bf16[64,2880]{1,0:T(8,128)(2,1)} collective-permute-done((bf16[64,2880]{1,0:T(8,128)(2,1)S(1)}, bf16[64,2880]{1,0:T(8,128)(2,1)}, u32[]{:S(2)}, u32[]{:S(2)}) %collective-permute-start.14) | collective-permute-done | bytes 368672 | tf_op jit(solution)/shard_map/ppermute | solution.py:29
  412.4 2.1 copy.203
  414.6 2.4 add_convert_fusion
  417.0 2.1 copy.204
  (94 shorter events, 13.9 us)
Async XLA Ops:
  0.0 7.6 %collective-permute-start.1 = (bf16[128,256]{1,0:T(8,128)(2,1)}, bf16[128,256]{1,0:T(8,128)(2,1)S(1)}, u32[]{:S(2)}, u32[]{:S(2)}) collective-permute-start(bf16[128,256]{1,0:T(8,128)(2,1)} %param.14), channel_id=1, source_target_pairs={{0,2},{2,4},{4,6},{6,8},{8,10},{10,12},{12,14},{14,16},{16,18},{18... | collective-permute-start | bytes 196616 | tf_op jit(solution)/shard_map/ppermute | solution.py:20
  1.9 6.6 %collective-permute-start = (bf16[128,256]{1,0:T(8,128)(2,1)}, bf16[128,256]{1,0:T(8,128)(2,1)S(1)}, u32[]{:S(2)}, u32[]{:S(2)}) collective-permute-start(bf16[128,256]{1,0:T(8,128)(2,1)} %param.15), channel_id=1, source_target_pairs={{0,2},{2,4},{4,6},{6,8},{8,10},{10,12},{12,14},{14,16},{16,18},{18... | collective-permute-start | bytes 196616 | tf_op jit(solution)/shard_map/ppermute | solution.py:20
  10.1 2.2 slice-start
  10.7 2.3 slice-start.1
  12.9 3.9 copy-start.13
  15.2 10.7 %collective-permute-start.2 = (bf16[64,2880]{1,0:T(8,128)(2,1)S(1)}, bf16[64,2880]{1,0:T(8,128)(2,1)S(1)}, u32[]{:S(2)}, u32[]{:S(2)}) collective-permute-start(bf16[64,2880]{1,0:T(8,128)(2,1)S(1)} %copy.209), channel_id=1, source_target_pairs={{0,1},{1,0},{2,3},{3,2},{4,5},{5,4},{6,7},{7,6},{8,9},{9,8},{10,11... | collective-permute-start | bytes 1105928 | tf_op jit(solution)/shard_map/ppermute | solution.py:29
  18.0 11.0 %copy-start.14 = (f32[2880]{0:T(1024)S(1)}, f32[2880]{0:T(1024)}, u32[]{:S(2)}) copy-start(f32[2880]{0:T(1024)} %param.18) | copy-start | bytes 34564
  28.9 43.3 %copy-start = (f32[64,2880]{0,1:T(8,128)}, f32[64,2880]{0,1:T(8,128)S(1)}, u32[]{:S(2)}) copy-start(f32[64,2880]{0,1:T(8,128)S(1)} %get-tuple-element.8) | copy-start | bytes 2211844
  30.4 11.9 %collective-permute-start.6 = (bf16[64,2880]{1,0:T(8,128)(2,1)}, bf16[64,2880]{1,0:T(8,128)(2,1)S(1)}, u32[]{:S(2)}, u32[]{:S(2)}) collective-permute-start(bf16[64,2880]{1,0:T(8,128)(2,1)} %copy.159), channel_id=1, source_target_pairs={{0,8},{2,10},{4,12},{6,14},{8,16},{10,18},{12,20},{14,22},{16,24},... | collective-permute-start | bytes 1105928 | tf_op jit(solution)/shard_map/ppermute | solution.py:20
  33.9 11.9 %collective-permute-start.3 = (bf16[64,2880]{1,0:T(8,128)(2,1)}, bf16[64,2880]{1,0:T(8,128)(2,1)S(1)}, u32[]{:S(2)}, u32[]{:S(2)}) collective-permute-start(bf16[64,2880]{1,0:T(8,128)(2,1)} %copy.159), channel_id=1, source_target_pairs={{8,0},{10,2},{12,4},{14,6},{16,8},{18,10},{20,12},{22,14},{24,16},... | collective-permute-start | bytes 1105928 | tf_op jit(solution)/shard_map/ppermute | solution.py:20
  42.3 11.0 %collective-permute-start.7 = (bf16[64,2880]{1,0:T(8,128)(2,1)S(1)}, bf16[64,2880]{1,0:T(8,128)(2,1)}, u32[]{:S(2)}, u32[]{:S(2)}) collective-permute-start(bf16[64,2880]{1,0:T(8,128)(2,1)S(1)} %collective-permute-done.6), channel_id=1, source_target_pairs={{0,8},{2,10},{4,12},{6,14},{8,16},{10,18},{12,20},{14,22},{16,24},... | collective-permute-start | bytes 1105928 | tf_op jit(solution)/shard_map/ppermute | solution.py:20
  45.8 10.9 %collective-permute-start.4 = (bf16[64,2880]{1,0:T(8,128)(2,1)S(1)}, bf16[64,2880]{1,0:T(8,128)(2,1)}, u32[]{:S(2)}, u32[]{:S(2)}) collective-permute-start(bf16[64,2880]{1,0:T(8,128)(2,1)S(1)} %collective-permute-done.3), channel_id=1, source_target_pairs={{8,0},{10,2},{12,4},{14,6},{16,8},{18,10},{20,12},{22,14},{24,16},... | collective-permute-start | bytes 1105928 | tf_op jit(solution)/shard_map/ppermute | solution.py:20
  53.3 11.9 %collective-permute-start.8 = (bf16[64,2880]{1,0:T(8,128)(2,1)}, bf16[64,2880]{1,0:T(8,128)(2,1)}, u32[]{:S(2)}, u32[]{:S(2)}) collective-permute-start(bf16[64,2880]{1,0:T(8,128)(2,1)} %collective-permute-done.7), channel_id=1, source_target_pairs={{0,8},{2,10},{4,12},{6,14},{8,16},{10,18},{12,20},{14,22},{16,24},... | collective-permute-start | bytes 1105928 | tf_op jit(solution)/shard_map/ppermute | solution.py:20
  56.8 10.5 %collective-permute-start.5 = (bf16[64,2880]{1,0:T(8,128)(2,1)}, bf16[64,2880]{1,0:T(8,128)(2,1)}, u32[]{:S(2)}, u32[]{:S(2)}) collective-permute-start(bf16[64,2880]{1,0:T(8,128)(2,1)} %collective-permute-done.4), channel_id=1, source_target_pairs={{8,0},{10,2},{12,4},{14,6},{16,8},{18,10},{20,12},{22,14},{24,16},... | collective-permute-start | bytes 1105928 | tf_op jit(solution)/shard_map/ppermute | solution.py:20
  69.5 2.8 copy-start.8
  69.5 2.8 copy-start.9
  69.5 2.8 copy-start.10
  69.5 2.9 copy-start.11
  81.9 15.9 %collective-permute-start.9 = (bf16[4,32,2880]{2,1,0:T(8,128)(2,1)}, bf16[4,32,2880]{2,1,0:T(8,128)(2,1)}, u32[]{:S(2)}, u32[]{:S(2)}) collective-permute-start(bf16[4,32,2880]{2,1,0:T(8,128)(2,1)} %copy.185), channel_id=1, source_target_pairs={{0,4},{2,6},{4,0},{6,2},{8,12},{10,14},{12,8},{14,10},{16,20},{18,... | collective-permute-start | bytes 2211848 | tf_op jit(solution)/shard_map/ppermute | solution.py:25
  86.0 15.7 %collective-permute-start.11 = (bf16[4,32,2880]{2,1,0:T(8,128)(2,1)}, bf16[4,32,2880]{2,1,0:T(8,128)(2,1)}, u32[]{:S(2)}, u32[]{:S(2)}) collective-permute-start(bf16[4,32,2880]{2,1,0:T(8,128)(2,1)} %copy.190), channel_id=1, source_target_pairs={{0,1},{1,0},{2,3},{3,2},{4,5},{5,4},{6,7},{7,6},{8,9},{9,8},{10,11... | collective-permute-start | bytes 2211848 | tf_op jit(solution)/shard_map/ppermute | solution.py:29
  112.5 4.0 copy-start.3
  119.0 8.5 %copy-start.2 = (bf16[1,4,32,2880]{2,3,1,0:T(8,128)(2,1)S(1)}, bf16[1,4,32,2880]{2,3,1,0:T(8,128)(2,1)}, u32[]{:S(2)}) copy-start(bf16[1,4,32,2880]{2,3,1,0:T(8,128)(2,1)} %get-tuple-element.14) | copy-start | bytes 2211844
  121.9 31.2 %collective-permute-start.12 = (bf16[2,4,32,2880]{3,2,1,0:T(8,128)(2,1)}, bf16[2,4,32,2880]{3,2,1,0:T(8,128)(2,1)}, u32[]{:S(2)}, u32[]{:S(2)}) collective-permute-start(bf16[2,4,32,2880]{3,2,1,0:T(8,128)(2,1)} %pad_maximum_fusion.4), channel_id=1, source_target_pairs={{0,4},{2,6},{4,0},{6,2},{8,12},{10,14},{12,8},{14,10},{16,20},{18,... | collective-permute-start | bytes 4423688 | tf_op jit(solution)/shard_map/ppermute | solution.py:25
  130.0 23.1 %copy-start.6 = (bf16[1,4,32,2880]{3,2,1,0:T(8,128)(2,1)S(1)}, bf16[1,4,32,2880]{3,2,1,0:T(8,128)(2,1)}, u32[]{:S(2)}) copy-start(bf16[1,4,32,2880]{3,2,1,0:T(8,128)(2,1)} %copy.194) | copy-start | bytes 2211844
  130.0 23.1 %copy-start.7 = (bf16[1,4,32,2880]{3,2,1,0:T(8,128)(2,1)S(1)}, bf16[1,4,32,2880]{3,2,1,0:T(8,128)(2,1)}, u32[]{:S(2)}) copy-start(bf16[1,4,32,2880]{3,2,1,0:T(8,128)(2,1)} %copy.193) | copy-start | bytes 2211844
  131.6 30.4 %collective-permute-start.10 = (bf16[2,4,32,2880]{3,2,1,0:T(8,128)(2,1)S(1)}, bf16[2,4,32,2880]{3,2,1,0:T(8,128)(2,1)S(1)}, u32[]{:S(2)}, u32[]{:S(2)}) collective-permute-start(bf16[2,4,32,2880]{3,2,1,0:T(8,128)(2,1)S(1)} %pad_maximum_fusion.3), channel_id=1, source_target_pairs={{0,1},{1,0},{2,3},{3,2},{4,5},{5,4},{6,7},{7,6},{8,9},{9,8},{10,11... | collective-permute-start | bytes 4423688 | tf_op jit(solution)/shard_map/ppermute | solution.py:29
  154.9 7.2 %copy-start.4 = (bf16[1,4,32,2880]{3,2,1,0:T(8,128)(2,1)S(1)}, bf16[1,4,32,2880]{3,2,1,0:T(8,128)(2,1)}, u32[]{:S(2)}) copy-start(bf16[1,4,32,2880]{3,2,1,0:T(8,128)(2,1)} %copy.188) | copy-start | bytes 2211844
  154.9 7.2 %copy-start.5 = (bf16[1,4,32,2880]{3,2,1,0:T(8,128)(2,1)S(1)}, bf16[1,4,32,2880]{3,2,1,0:T(8,128)(2,1)}, u32[]{:S(2)}) copy-start(bf16[1,4,32,2880]{3,2,1,0:T(8,128)(2,1)} %copy.189) | copy-start | bytes 2211844
  166.2 8.4 %copy-start.15 = (s32[128,4]{0,1:T(4,128)S(1)}, s32[128,4]{0,1:T(4,128)}, u32[]{:S(2)}) copy-start(s32[128,4]{0,1:T(4,128)} %param.22) | copy-start | bytes 6148
  166.2 8.4 %copy-start.16 = (f32[128,4]{0,1:T(4,128)S(1)}, f32[128,4]{0,1:T(4,128)}, u32[]{:S(2)}) copy-start(f32[128,4]{0,1:T(4,128)} %param.23) | copy-start | bytes 6148
  174.6 29.7 %collective-permute-start.13 = (bf16[8,128,2880]{1,2,0:T(8,128)(2,1)}, bf16[8,128,2880]{1,2,0:T(8,128)(2,1)}, u32[]{:S(2)}, u32[]{:S(2)}) collective-permute-start(bf16[8,128,2880]{1,2,0:T(8,128)(2,1)} %copy.198), channel_id=1, source_target_pairs={{0,2},{2,0},{4,6},{6,4},{8,10},{10,8},{12,14},{14,12},{16,18},{18,... | collective-permute-start | bytes 17694728 | tf_op jit(solution)/shard_map/ppermute | solution.py:25
  194.4 16.1 %slice-start.2 = ((s8[4423680]{0:T(1024)(128)(4,1)}), s8[4194304]{0:T(1024)(128)(4,1)S(1)}, s32[]{:S(2)}) async-start(s8[4423680]{0:T(1024)(128)(4,1)} %bitcast.140), calls=%async_computation.3 | async-start | bytes 8388608
  198.2 12.3 %slice-start.3 = ((s8[4423680]{0:T(1024)(128)(4,1)}), s8[229376]{0:T(1024)(128)(4,1)S(1)}, s32[]{:S(2)}) async-start(s8[4423680]{0:T(1024)(128)(4,1)} %bitcast.140), calls=%async_computation.4 | async-start | bytes 458752
  208.9 1.6 copy-start.12
  251.8 141.7 %all-to-all-start = ((bf16[16,64,2880]{2,1,0:T(8,128)(2,1)}), bf16[16,64,2880]{2,1,0:T(8,128)(2,1)}, u32[]{:S(2)}, u32[]{:S(2)}) async-start(bf16[16,64,2880]{2,1,0:T(8,128)(2,1)} %bitcast.122), calls=%async_computation | async-start | bytes 12058624 | tf_op jit(solution)/shard_map/all_to_all | solution.py:164
  398.7 15.9 %copy-start.1 = (f32[64,2880]{0,1:T(8,128)S(1)}, f32[64,2880]{0,1:T(8,128)}, u32[]{:S(2)}) copy-start(f32[64,2880]{0,1:T(8,128)} %copy-done) | copy-start | bytes 2211844
  401.2 11.2 %collective-permute-start.14 = (bf16[64,2880]{1,0:T(8,128)(2,1)S(1)}, bf16[64,2880]{1,0:T(8,128)(2,1)}, u32[]{:S(2)}, u32[]{:S(2)}) collective-permute-start(bf16[64,2880]{1,0:T(8,128)(2,1)S(1)} %copy.210), channel_id=1, source_target_pairs={{0,1},{1,0},{2,3},{3,2},{4,5},{5,4},{6,7},{7,6},{8,9},{9,8},{10,11... | collective-permute-start | bytes 1105928 | tf_op jit(solution)/shard_map/ppermute | solution.py:29
